TPU v7x, 32 devices: a whole 2x2x4 slice. The times are simulated.
32 devices in a mesh: grp: 4 (over y, core), shard: 8 (over z, x).
Axes of the slice: x: 2, y: 2, z: 4, core: 2. Of those that a mesh axis runs over, the one named last changes fastest.
Arguments:
- queries: bfloat16 [8192, 256], P(('grp', 'shard')), may hold values from -6 to 6
- positive: int32 [8192], P(('grp', 'shard')), may hold values from 0 to 255
- item_feats: bfloat16 [8192, 128], P(('grp', 'shard')), may hold values from -6 to 6
- frequency: int32 [8192], P(('grp', 'shard')), may hold values from 0 to 1048575
- samples: int32 [32, 8, 128], P(('grp', 'shard')), may hold values from 0 to 255
- counts: int32 [32, 8], P(('grp', 'shard')), may hold values from 1 to 128, as said below
- w_in: bfloat16 [128, 4096], replicated, may hold values from -0.5 to 0.5
- w_out: bfloat16 [4096, 256], replicated, may hold values from -0.09375 to 0.09375
Outputs:
- query_grad: float32 [8192, 256], P(('grp', 'shard'))
- w_in_grad: float32 [128, 4096], P(None, 'shard')
- w_out_grad: float32 [4096, 256], P('shard')
Inputs may be any that keep to these rules, and one draw needn't show every extreme that they name: samples[d, s, k] is a row of the item block of device s of d's group; slots k >= counts[d, s] are ignored. `counts`: in every group one device receives 128 live rows from every source. `positive`: a row of the query's own device's item block.
All inputs are finite; a program needn't handle non-finite values.
Results may differ from a plain program's by a relative error of at most 0.019.
Values may be sent and summed in bfloat16 or wider, within the bound.
A program may use at most 64 MiB of HBM per device.

v0:
```python
import jax
import jax.numpy as jnp
from jax import lax
from jax.sharding import PartitionSpec as P

logit_divisor_factor = 0.05
log_base = 4.0
epsilon = 1e-06
masked_logit = -10000.0


def contract_rows(left, right):
    return lax.dot_general(
        left, right, (((0,), (0,)), ((), ())), preferred_element_type=jnp.float32
    )


def item_tower(feats, w_in, w_out, freqs):
    preact = jnp.dot(feats, w_in, preferred_element_type=jnp.float32)
    hidden = jnp.maximum(preact, 0.0).astype(jnp.bfloat16)
    raw_emb = jnp.dot(hidden, w_out, preferred_element_type=jnp.float32)
    radius = jnp.sqrt(jnp.sum(raw_emb * raw_emb, -1, keepdims=True) + epsilon)
    unit_emb = raw_emb / radius
    log_bias = (log_base - jnp.log(freqs.astype(jnp.float32) + 1.0)).astype(jnp.bfloat16)
    return (preact, hidden, radius, unit_emb, log_bias)


def query_side(query_rows, pos_local, own_units, contrast_drawn_item, neg_bias, live_slot):
    query_f = query_rows.astype(jnp.float32)
    query_norm = jnp.sqrt(jnp.sum(query_f * query_f, -1, keepdims=True) + epsilon)
    query_unit = query_f / query_norm
    request_vector_narrow = query_unit.astype(jnp.bfloat16)
    matched_entry_list = jnp.take(own_units, pos_local, axis=0)
    matched_logit_value = (
        jnp.sum(
            request_vector_narrow.astype(jnp.float32) * matched_entry_list.astype(jnp.float32), -1
        )
        / logit_divisor_factor
    )
    whole_offset_vector = jnp.where(live_slot, neg_bias.astype(jnp.float32), masked_logit)
    contrast_logit_value = (
        lax.dot_general(
            request_vector_narrow,
            contrast_drawn_item,
            (((1,), (1,)), ((), ())),
            preferred_element_type=jnp.float32,
        )
        / logit_divisor_factor
        + whole_offset_vector[None, :]
    )
    neg_exp = jnp.exp(contrast_logit_value)
    pos_exp = jnp.exp(matched_logit_value)
    total = pos_exp + jnp.sum(neg_exp, -1)
    contrast_probability = neg_exp / total[:, None]
    matched_probability = pos_exp / total
    contrast_derivative = (contrast_probability / logit_divisor_factor).astype(jnp.bfloat16)
    matched_derivative = (matched_probability - 1.0) / logit_divisor_factor
    unit_qgrad = jnp.dot(
        contrast_derivative, contrast_drawn_item, preferred_element_type=jnp.float32
    ) + matched_derivative[:, None] * matched_entry_list.astype(jnp.float32)
    query_grad = (
        unit_qgrad - query_unit * jnp.sum(query_unit * unit_qgrad, -1, keepdims=True)
    ) / query_norm
    row_grad = contract_rows(contrast_derivative, request_vector_narrow).astype(jnp.bfloat16)
    pos_sum = jax.ops.segment_sum(
        matched_derivative[:, None] * request_vector_narrow.astype(jnp.float32),
        pos_local,
        num_segments=own_units.shape[0],
    )
    return (query_grad, row_grad, pos_sum)


def tower_back(feats, w_out, preact, hidden, radius, unit_emb, item_grad):
    raw_grad = (
        (item_grad - unit_emb * jnp.sum(unit_emb * item_grad, -1, keepdims=True)) / radius
    ).astype(jnp.bfloat16)
    w_out_part = contract_rows(hidden, raw_grad)
    hid_grad = lax.dot_general(
        raw_grad, w_out, (((1,), (1,)), ((), ())), preferred_element_type=jnp.float32
    )
    pre_grad = jnp.where(preact > 0.0, hid_grad, 0.0).astype(jnp.bfloat16)
    w_in_part = contract_rows(feats, pre_grad)
    return (w_in_part, w_out_part)


def local(queries, positive, item_feats, frequency, samples, counts, w_in, w_out):
    peer_count = lax.axis_size("shard")
    slot_count = samples.shape[2]
    item_count = item_feats.shape[0]
    emb_width = w_out.shape[1]
    preact, hidden, radius, unit_emb, log_bias = item_tower(item_feats, w_in, w_out, frequency)
    unit_bf = unit_emb.astype(jnp.bfloat16)
    own_samples = samples[0]
    requests = lax.all_to_all(own_samples, "shard", split_axis=0, concat_axis=0, tiled=True)
    group_rows, group_bias = (
        lax.all_gather(unit_bf, "shard", axis=0, tiled=True),
        lax.all_gather(log_bias, "shard", axis=0, tiled=True),
    )
    flat_index = (
        jnp.arange(peer_count, dtype=jnp.int32)[:, None] * item_count + own_samples
    ).reshape(-1)
    contrast_drawn_item = jnp.take(group_rows, flat_index, axis=0)
    neg_bias = jnp.take(group_bias, flat_index, axis=0)
    live_slot = (jnp.arange(slot_count, dtype=jnp.int32)[None, :] < counts[0][:, None]).reshape(-1)
    query_grad, row_grad, pos_sum = query_side(
        queries, positive, unit_bf, contrast_drawn_item, neg_bias, live_slot
    )
    returned = lax.all_to_all(
        row_grad.reshape(peer_count, slot_count, emb_width),
        "shard",
        split_axis=0,
        concat_axis=0,
        tiled=True,
    )
    item_grad = jax.ops.segment_sum(
        returned.reshape(-1, emb_width).astype(jnp.float32),
        requests.reshape(-1),
        num_segments=item_count,
    )
    item_grad = item_grad + pos_sum
    w_in_part, w_out_part = tower_back(
        item_feats, w_out, preact, hidden, radius, unit_emb, item_grad
    )
    w_in_share, w_out_share = (
        lax.psum_scatter(
            w_in_part.astype(jnp.bfloat16), "shard", scatter_dimension=1, tiled=True
        ).astype(jnp.float32),
        lax.psum_scatter(
            w_out_part.astype(jnp.bfloat16), "shard", scatter_dimension=0, tiled=True
        ).astype(jnp.float32),
    )
    w_in_grad, w_out_grad = (
        lax.psum(w_in_share.astype(jnp.bfloat16), "grp").astype(jnp.float32),
        lax.psum(w_out_share.astype(jnp.bfloat16), "grp").astype(jnp.float32),
    )
    return (query_grad, w_in_grad, w_out_grad)


def solution(mesh):
    in_specs = (
        P(("grp", "shard"), None),
        P(("grp", "shard")),
        P(("grp", "shard"), None),
        P(("grp", "shard")),
        P(("grp", "shard"), None, None),
        P(("grp", "shard"), None),
        P(),
        P(),
    )
    out_specs = (P(("grp", "shard"), None), P(None, "shard"), P("shard", None))
    return jax.shard_map(local, mesh=mesh, in_specs=in_specs, out_specs=out_specs, check_vma=False)
```

profile of v0, /device:TPU:0, one launch (start us, length us, event | category | flops | bytes accessed | tf_op | source)
XLA Modules:
  0.0 271.1 jit_solution(5464032628026734501)
XLA Ops:
  7.2 2.1 fusion.24
  9.4 1.1 multiply_reduce_fusion.2
  12.0 7.3 %all-to-all-start = ((s32[8,1,128]{2,1,0:T(1,128)}), s32[8,1,128]{2,1,0:T(1,128)}, u32[]{:S(2)}, u32[]{:S(2)}) async-start(s32[8,1,128]{2,1,0:T(1,128)} %bitcast.7), calls=%async_computation | async-start | bytes 8192 | tf_op jit(solution)/shard_map/all_to_all | solution.py:94
  20.3 1.2 gather_fusion.2
  21.7 21.0 %all-gather = bf16[8,1,256]{2,1,0:T(2,128)(2,1)S(1)} all-gather(bf16[1,1,256]{2,1,0:T(2,128)(2,1)S(1)} %reshape.170), channel_id=1, replica_groups=mesh['grp'=4,'shard'=8] {'shard'}, dimensions={0}, use_global_device_ids=true | all-gather | bytes 4608 | tf_op jit(solution)/shard_map/all_gather | solution.py:97
  43.6 6.8 %gather_fusion.1 = bf16[1024]{0:T(1024)(128)(2,1)S(1)} fusion(bf16[2048]{0:T(1024)(128)(2,1)S(1)} %bitcast.36, s32[1024]{0:T(1024)S(1)} %broadcast_clamp_fusion), kind=kCustom, calls=%fused_computation.1 | custom fusion | bytes 8192 | tf_op jit(solution)/shard_map/jit(_take)/gather | solution.py:103
  50.5 1.4 convert_select_fusion
  51.9 2.7 all-gather.3.cloned.1.call-done
  54.6 1.5 copy.28
  56.1 5.0 %gather_fusion = bf16[1024,256]{1,0:T(8,128)(2,1)} fusion(bf16[2048,256]{1,0:T(8,128)(2,1)S(1)} %copy.28, s32[1024]{0:T(1024)S(1)} %broadcast_clamp_fusion), kind=kCustom, calls=%fused_computation | custom fusion | bytes 1052672 | tf_op jit(solution)/shard_map/jit(_take)/gather | solution.py:102
  61.0 1.7 fusion.23
  63.7 1.2 convolution_convert_fusion.2
  64.9 3.5 %all-to-all-start.1 = ((bf16[8,128,256]{2,1,0:T(8,128)(2,1)}), bf16[8,128,256]{2,1,0:T(8,128)(2,1)S(1)}, u32[]{:S(2)}, u32[]{:S(2)}) async-start(bf16[8,128,256]{2,1,0:T(8,128)(2,1)} %bitcast.9), calls=%async_computation.1 | async-start | bytes 1048576 | tf_op jit(solution)/shard_map/all_to_all | solution.py:108
  68.5 2.5 convert_multiply_fusion.2
  71.8 2.4 scatter_custom_fusion.1
  74.4 8.2 %all-to-all-done.1 = bf16[8,128,256]{2,1,0:T(8,128)(2,1)S(1)} async-done(((bf16[8,128,256]{2,1,0:T(8,128)(2,1)}), bf16[8,128,256]{2,1,0:T(8,128)(2,1)S(1)}, u32[]{:S(2)}, u32[]{:S(2)}) %all-to-all-start.1) | async-done | bytes 524320 | tf_op jit(solution)/shard_map/all_to_all | solution.py:108
  82.5 6.3 %scatter_custom_fusion = f32[256,256]{1,0:T(8,128)S(1)} fusion(s32[1024]{0:T(1024)} %bitcast.8, bf16[1024,256]{1,0:T(8,128)(2,1)S(1)} %bitcast.37, f32[]{:T(128)} %constant.35.clone.1), kind=kCustom, calls=%fused_computation.16 | custom fusion | flops 524288 | bytes 786944 | tf_op jit(solution)/shard_map/scatter-add | solution.py:115
  89.1 4.5 %fusion.1 = bf16[128,4096]{0,1:T(8,128)(2,1)} fusion(bf16[256,128]{1,0:T(8,128)(2,1)} %param.10, bf16[4096,256]{1,0:T(8,128)(2,1)S(1)} %copy-done, f32[256,4096]{1,0:T(8,128)} %copy-done.1, f32[256,256]{0,1:T(8,128)S(1)} %get-tuple-element.15, f32[256]{0:T(256)S(1)} %get-tuple-element.14, f32[256]{0:T(256)S(1)} %add_sqrt_fusion, ...), kind=kOutput, calls=%fused_computation.9 | convolution fusion | flops 809304064 | bytes 7931904 | tf_op jit(solution)/shard_map/dot_general | solution.py:13
  93.6 4.3 %convolution_convert_fusion = bf16[4096,256]{1,0:T(8,128)(2,1)} fusion(f32[256,4096]{1,0:T(8,128)} %copy-done.1, f32[256,256]{0,1:T(8,128)S(1)} %get-tuple-element.15, f32[256]{0:T(256)S(1)} %get-tuple-element.14, f32[256]{0:T(256)S(1)} %add_sqrt_fusion, f32[256,256]{0,1:T(8,128)S(1)} %get-tuple-element.23), kind=kOutput, calls=%fused_computation.7 | convolution fusion | flops 540344320 | bytes 6817792 | tf_op jit(solution)/shard_map/dot_general | solution.py:13
  98.0 58.2 %reduce-scatter.3.cloned.1.call-done = bf16[128,512]{0,1:T(8,128)(2,1)} async-done(((bf16[128,4096]{0,1:T(8,128)(2,1)}), bf16[128,512]{0,1:T(8,128)(2,1)}) %reduce-scatter.3.cloned.1.call-update) | async-done | bytes 131088 | tf_op jit(solution)/shard_map/reduce_scatter | solution.py:125
  156.2 70.6 %reduce-scatter.5.cloned.1.call-done = bf16[512,256]{1,0:T(8,128)(2,1)} async-done(((bf16[4096,256]{1,0:T(8,128)(2,1)}), bf16[512,256]{1,0:T(8,128)(2,1)}) %reduce-scatter.5.cloned.1.call-update) | async-done | bytes 262160 | tf_op jit(solution)/shard_map/reduce_scatter | solution.py:128
  227.8 33.3 %all-reduce.3.cloned.1.call-done = (bf16[128,512]{0,1:T(8,128)(2,1)}, bf16[512,256]{1,0:T(8,128)(2,1)}) async-done(((bf16[128,512]{0,1:T(8,128)(2,1)}, bf16[512,256]{1,0:T(8,128)(2,1)}), (bf16[128,512]{0,1:T(8,128)(2,1)}, bf16[512,256]{1,0:T(8,128)(2,1)})) %all-reduce.3.cloned.1.call-update) | async-done | bytes 393232 | tf_op jit(solution)/shard_map/psum | solution.py:133
  261.1 1.7 copy.35
  262.8 1.8 convert_element_type.89
  (62 shorter events, 7.1 us)
Async XLA Ops:
  7.2 2.2 copy-start
  7.2 47.4 %all-gather.3.cloned.1.call-start = ((), (), s32[]{:S(2)}) async-start(), calls=%async_computation.4 | async-start | bytes 1179648 | tf_op jit(solution)/shard_map/all_gather | solution.py:96
  9.3 1.9 copy-start.1
  9.3 10.9 %copy-start.8 = (s32[256]{0:T(256)S(1)}, s32[256]{0:T(256)}, u32[]{:S(2)}) copy-start(s32[256]{0:T(256)} %param.9) | copy-start | bytes 3076
  11.3 10.3 %copy-start.6 = (bf16[256,256]{1,0:T(8,128)(2,1)S(1)}, bf16[256,256]{1,0:T(8,128)(2,1)}, u32[]{:S(2)}) copy-start(bf16[256,256]{1,0:T(8,128)(2,1)} %param.8) | copy-start | bytes 393220
  11.3 10.4 %copy-start.12 = (s32[256]{0:T(256)S(1)}, s32[256]{0:T(256)}, u32[]{:S(2)}) copy-start(s32[256]{0:T(256)} %param.11) | copy-start | bytes 3076
  12.0 52.9 %all-to-all-start = ((s32[8,1,128]{2,1,0:T(1,128)}), s32[8,1,128]{2,1,0:T(1,128)}, u32[]{:S(2)}, u32[]{:S(2)}) async-start(s32[8,1,128]{2,1,0:T(1,128)} %bitcast.7), calls=%async_computation | async-start | bytes 8192 | tf_op jit(solution)/shard_map/all_to_all | solution.py:94
  20.3 30.3 %copy-start.11 = (s32[1,8]{1,0:T(1,128)S(1)}, s32[1,8]{1,0:T(1,128)}, u32[]{:S(2)}) copy-start(s32[1,8]{1,0:T(1,128)} %param.13) | copy-start | bytes 100
  21.6 30.3 %copy-start.2 = (bf16[256,256]{0,1:T(8,128)(2,1)}, bf16[256,256]{0,1:T(8,128)(2,1)S(1)}, u32[]{:S(2)}) copy-start(bf16[256,256]{0,1:T(8,128)(2,1)S(1)} %copy.30) | copy-start | bytes 393220
  50.4 1.5 copy-start.9
  62.7 5.7 %copy-start.3 = (bf16[256,256]{0,1:T(8,128)(2,1)S(1)}, bf16[256,256]{0,1:T(8,128)(2,1)}, u32[]{:S(2)}) copy-start(bf16[256,256]{0,1:T(8,128)(2,1)} %copy-done.2) | copy-start | bytes 393220
  62.7 5.7 %copy-start.7 = (pred[1024]{0:T(1024)(128)(4,1)S(1)}, pred[1024]{0:T(1024)(128)(4,1)}, u32[]{:S(2)}) copy-start(pred[1024]{0:T(1024)(128)(4,1)} %get-tuple-element.17) | copy-start | bytes 3076
  62.7 5.7 %copy-start.10 = (pred[256]{0:T(512)(128)(4,1)S(1)}, pred[256]{0:T(512)(128)(4,1)}, u32[]{:S(2)}) copy-start(pred[256]{0:T(512)(128)(4,1)} %copy-done.9) | copy-start | bytes 772
  62.9 0.8 copy-start.4
  64.9 17.6 %all-to-all-start.1 = ((bf16[8,128,256]{2,1,0:T(8,128)(2,1)}), bf16[8,128,256]{2,1,0:T(8,128)(2,1)S(1)}, u32[]{:S(2)}, u32[]{:S(2)}) async-start(bf16[8,128,256]{2,1,0:T(8,128)(2,1)} %bitcast.9), calls=%async_computation.1 | async-start | bytes 1048576 | tf_op jit(solution)/shard_map/all_to_all | solution.py:108
  68.4 87.8 %reduce-scatter.3.cloned.1.call-start = ((), (), s32[]{:S(2)}) async-start(), calls=%async_computation.5 | async-start | bytes 1179648 | tf_op jit(solution)/shard_map/reduce_scatter | solution.py:125
  93.6 133.3 %reduce-scatter.5.cloned.1.call-start = ((), (), s32[]{:S(2)}) async-start(), calls=%async_computation.6 | async-start | bytes 2359296 | tf_op jit(solution)/shard_map/reduce_scatter | solution.py:128
  97.9 129.0 %copy-start.5 = (f32[256,256]{0,1:T(8,128)S(1)}, f32[256,256]{0,1:T(8,128)}, u32[]{:S(2)}) copy-start(f32[256,256]{0,1:T(8,128)} %get-tuple-element.26) | copy-start | bytes 786436
  98.0 163.2 %all-reduce.3.cloned.1.call-start = ((), (), s32[]{:S(2)}) async-start(), calls=%async_computation.7 | async-start | bytes 786432 | tf_op jit(solution)/shard_map/psum | solution.py:133
Sparse Core Ops, SparseCore 0:
  12.1 42.4 all-gather.2
  93.7 62.4 reduce-scatter.2
  160.2 66.6 reduce-scatter.4
  229.3 31.7 all-reduce.2
where the time goes:
time: 272 us; the launch traced here: 271 us
  waiting for transfers between devices  173 us (64%)
  local copies, waits for them, and re-layouts  21 us (8%)
  blocking collectives  21 us (8%)
  matrix products  17.2 us (6%)
  between operations  14.1 us (5%)
  other arithmetic  13.8 us (5%)
  starting transfers between devices  10.9 us (4%)
    reduce_scatter x1, waiting for transfers between devices, local(): lax.psum_scatter(w_out_part.astype(jnp.bfloat16), 'shard', scatter_dimens...  70.6 us
    reduce_scatter x1, waiting for transfers between devices, local(): lax.psum_scatter(w_in_part.astype(jnp.bfloat16), 'shard', scatter_dimensi...  58.2 us
    psum x1, waiting for transfers between devices, local(): lax.psum(w_in_share.astype(jnp.bfloat16), 'grp').astype(jnp.float32)  33.3 us
    all_gather x1, blocking collectives, local(): lax.all_gather(log_bias, 'shard', axis=0, tiled=True)  21 us
    dot_general x3, matrix products, contract_rows(): lax.dot_general(left, right, (((0,), (0,)), ((), ())), preferred_element_...  9.95 us
    all_to_all x1, waiting for transfers between devices, local(): lax.all_to_all(row_grad.reshape(peer_count, slot_count, emb_width), 'shar...  8.17 us
    all_to_all x1, starting transfers between devices, local(): lax.all_to_all(own_samples, 'shard', split_axis=0, concat_axis=0, tiled=T...  7.26 us
    gather x1, local copies, waits for them, and re-layouts, local(): neg_bias = jnp.take(group_bias, flat_index, axis=0)  6.8 us
  transfers between devices with their start and end apart: 6, of which 5 were waited for; matrix products, arithmetic and copies ran while one was open for 12% of the time, Pallas kernels for 0%

commit v1 on v0

v1 whole, which is shorter than its diff:
```python
import functools
import math

import jax
import jax.numpy as jnp
from jax import lax
from jax.experimental import pallas as pl
from jax.experimental.pallas import tpu as pltpu
from jax.sharding import PartitionSpec as P

inv_temperature = 1.0 / 0.05
log_base = 4.0
epsilon = 1e-06
masked_logit = -10000.0
MESH = pl.DeviceIdType.MESH
F32 = jnp.float32
BF16 = jnp.bfloat16


def mm(left, right, dims):
    return lax.dot_general(left, right, (dims, ((), ())), preferred_element_type=F32)


NN = ((1,), (0,))
NT = ((1,), (1,))
TN = ((0,), (0,))


def kernel(
    dims,
    q_ref, pos_ref, feats_ref, freq_ref, samp_ref, counts_ref, w_in_ref, w_out_ref,
    qg_ref, wig_ref, wog_ref,
    req, fsend, frecv, ngrad, esc, tot, rsend, rrecv, hid, hidt, acc, uq, part, crecv,
    a1, r1y, b1, r1x, c1, r1z,
    a2, r2x, b2, r2y, c2, r2z,
    fin, gath, tmp,
    req_s, req_r, fwd_s, fwd_r, bwd_s, bwd_r, core_s, core_r,
    y1_s, y1_r, x1_s, x1_r, z1_s, z1_r,
    x2_s, x2_r, y2_s, y2_r, z2_s, z2_r, ag_s, ag_r,
):
    n, ngrp, nx, nz, ny, rows = dims
    width = w_out_ref.shape[1]
    items = feats_ref.shape[0]
    slots = samp_ref.shape[2]
    cb = w_out_ref.shape[0] // n
    g = lax.axis_index("grp")
    me = lax.axis_index("shard")
    core, my_y = lax.rem(g, 2), lax.div(g, 2)
    my_x, my_z = lax.rem(me, nx), lax.div(me, nx)

    def shard_dev(p):
        return {"shard": p}

    def grp_dev(p):
        return {"grp": p}

    def y_dev(p):
        return {"grp": p * 2 + core}

    def x_dev(p):
        return {"shard": my_z * nx + p}

    def z_dev(p):
        return {"shard": p * nx + my_x}

    def remote(src, dst, ssem, rsem, dev):
        return pltpu.make_async_remote_copy(
            src_ref=src, dst_ref=dst, send_sem=ssem, recv_sem=rsem,
            device_id=dev, device_id_type=MESH,
        )

    barrier = pltpu.get_barrier_semaphore()
    for i in range(1, n):
        pl.semaphore_signal(
            barrier, inc=1, device_id=shard_dev(lax.rem(me + i, n)), device_id_type=MESH
        )
    for i in range(1, ngrp):
        pl.semaphore_signal(
            barrier, inc=1, device_id=grp_dev(lax.rem(g + i, ngrp)), device_id_type=MESH
        )
    pl.semaphore_wait(barrier, n - 1 + ngrp - 1)

    def req_copy(p, src):
        return remote(samp_ref.at[p], req.at[src], req_s.at[p], req_r.at[src], shard_dev(p))

    def fwd_copy(p, src):
        return remote(fsend.at[p], frecv.at[src], fwd_s.at[p], fwd_r.at[src], shard_dev(p))

    def bwd_copy(p, src):
        return remote(rsend.at[p], rrecv.at[src], bwd_s.at[p], bwd_r.at[src], shard_dev(p))

    def to(i):
        return lax.rem(me + i, n)

    def frm(i):
        return lax.rem(me + n - i, n)

    @pl.loop(1, n)
    def _(i):
        req_copy(to(i), me).start()

    req[pl.ds(me, 1)] = samp_ref[pl.ds(me, 1)]

    acc[...] = jnp.zeros_like(acc)

    @pl.loop(0, n)
    def _(b):
        cols = pl.ds(pl.multiple_of(b * cb, 128), cb)
        pre = mm(feats_ref[...], w_in_ref[:, cols], NN)
        h = jnp.maximum(pre, 0.0).astype(BF16)
        hid[b] = h
        acc[...] += mm(h, w_out_ref[cols, :], NN)

    raw_emb = acc[...]
    radius = jnp.sqrt(jnp.sum(raw_emb * raw_emb, -1, keepdims=True) + epsilon)
    unit = raw_emb / radius
    unit_bf = unit.astype(BF16)
    bias = (log_base - jnp.log(freq_ref[...].astype(F32) + 1.0)).astype(BF16)
    bias16 = jnp.broadcast_to(bias.astype(F32), (16, items)).astype(BF16)

    item_iota = lax.broadcasted_iota(jnp.int32, (items, slots), 0)

    def onehot(row):
        return (item_iota == row).astype(F32).astype(BF16)

    def gather_rows(buf, slot, src):
        pick = onehot(req[src])
        buf[slot, 0:slots, :] = mm(pick, unit_bf, TN).astype(BF16)
        b16 = mm(bias16, pick, NN).astype(BF16)
        for k in range(width // slots):
            buf[slot, slots : slots + 16, k * slots : (k + 1) * slots] = b16

    @pl.loop(1, n)
    def _(i):
        p = to(i)
        req_copy(p, p).wait_recv()
        gather_rows(fsend, p, p)
        fwd_copy(p, me).start()

    gather_rows(frecv, me, me)

    queries = q_ref[...].astype(F32)
    query_norm = jnp.sqrt(jnp.sum(queries * queries, -1, keepdims=True) + epsilon)
    query_unit = queries / query_norm
    query_bf = query_unit.astype(BF16)
    pos_pick = (
        lax.broadcasted_iota(jnp.int32, (items, q_ref.shape[0]), 0) == pos_ref[...]
    ).astype(F32).astype(BF16)
    pos_rows = mm(pos_pick, unit_bf, TN)
    pos_logit = jnp.sum(query_bf.astype(F32) * pos_rows, -1, keepdims=True) * inv_temperature
    pos_exp = jnp.exp(pos_logit)

    @pl.loop(0, n)
    def _(b):
        hidt[b] = hid[b].T

    slot_iota = lax.broadcasted_iota(jnp.int32, (1, slots), 1)

    def logits(src):
        off = frecv[src, slots : slots + 16, 0:slots].astype(F32)[0:1]
        off = jnp.where(slot_iota < counts_ref[0, src], off, masked_logit)
        z = mm(query_bf, frecv[src, 0:slots, :], NT) * inv_temperature + off
        e = jnp.exp(z)
        esc[src] = e
        return e

    tot[...] = logits(me)

    @pl.loop(1, n)
    def _(i):
        src = frm(i)
        fwd_copy(src, src).wait_recv()
        tot[...] += logits(src)

    total = pos_exp + jnp.sum(tot[...], -1, keepdims=True)
    scale = inv_temperature / total
    pos_grad = (pos_exp / total - 1.0) * inv_temperature

    def row_grads(src):
        d = (esc[src] * scale).astype(BF16)
        ngrad[src] = d
        return mm(d, query_bf, TN).astype(BF16)

    @pl.loop(1, n)
    def _(i):
        p = to(i)
        rsend[p] = row_grads(p)
        bwd_copy(p, me).start()

    rrecv[me] = row_grads(me)

    uq[...] = pos_grad * pos_rows

    @pl.loop(0, n)
    def _(b):
        uq[...] += mm(ngrad[b], frecv[b, 0:slots, :], NN)

    unit_qgrad = uq[...]
    qg_ref[...] = (
        unit_qgrad - query_unit * jnp.sum(query_unit * unit_qgrad, -1, keepdims=True)
    ) / query_norm

    pos_term = pos_grad * query_bf.astype(F32)
    high = pos_term.astype(BF16)
    low = (pos_term - high.astype(F32)).astype(BF16)
    acc[...] = mm(pos_pick, high, NN) + mm(pos_pick, low, NN)

    acc[...] += mm(onehot(req[me]), rrecv[me], NN)

    @pl.loop(1, n)
    def _(i):
        src = frm(i)
        bwd_copy(src, src).wait_recv()
        acc[...] += mm(onehot(req[src]), rrecv[src], NN)

    item_grad = acc[...]
    raw_grad = (
        (item_grad - unit * jnp.sum(unit * item_grad, -1, keepdims=True)) / radius
    ).astype(BF16)
    feats = feats_ref[...]

    def core_copy(b):
        return remote(
            part.at[b, 1 - core], crecv.at[b], core_s.at[b], core_r.at[b], grp_dev(g + 1 - 2 * core)
        )

    @pl.loop(0, n)
    def _(b):
        ht = hidt[b]
        wo = mm(ht, raw_grad, NN)
        hg = mm(w_out_ref[pl.ds(pl.multiple_of(b * cb, cb), cb), :], raw_grad, NT)
        pg = jnp.where(ht.astype(F32) > 0.0, hg, 0.0).astype(BF16)
        wi = mm(pg, feats, NN)
        for c in range(2):
            for y in range(ny):
                for h in range(2):
                    r0 = ((c * ny + y) * 2 + h) * rows
                    part[b, c, y, h, :, 0:width] = wo[r0 : r0 + rows].astype(BF16)
                    part[b, c, y, h, :, width:] = wi[r0 : r0 + rows].astype(BF16)
        core_copy(b).start()

    @pl.loop(0, n)
    def _(b):
        core_copy(b).wait_recv()
        bx, bz = lax.rem(b, nx), lax.div(b, nx)
        for y in range(ny):
            a1[y, bx, bz] = (
                part[b, core, y, 0].astype(F32) + crecv[b, y, 0].astype(F32)
            ).astype(BF16)
            a2[bx, y, bz] = (
                part[b, core, y, 1].astype(F32) + crecv[b, y, 1].astype(F32)
            ).astype(BF16)

    def exchange(count, mine, src, dst, ssem, rsem, dev):
        def copy(p, slot):
            return remote(src.at[p], dst.at[slot], ssem.at[p], rsem.at[slot], dev(p))

        def start():
            for i in range(1, count):
                copy(lax.rem(mine + i, count), mine).start()

        def wait_recv():
            for i in range(1, count):
                p = lax.rem(mine + i, count)
                copy(p, p).wait_recv()

        def wait_send():
            for i in range(1, count):
                copy(lax.rem(mine + i, count), mine).wait_send()

        def total_at(*index):
            value = src[(mine, *index)].astype(F32)
            for i in range(1, count):
                value += dst[(lax.rem(mine + i, count), *index)].astype(F32)
            return value.astype(BF16)

        return start, wait_recv, wait_send, total_at

    ex_y1 = exchange(ny, my_y, a1, r1y, y1_s, y1_r, y_dev)
    ex_x1 = exchange(nx, my_x, b1, r1x, x1_s, x1_r, x_dev)
    ex_z1 = exchange(nz, my_z, c1, r1z, z1_s, z1_r, z_dev)
    ex_x2 = exchange(nx, my_x, a2, r2x, x2_s, x2_r, x_dev)
    ex_y2 = exchange(ny, my_y, b2, r2y, y2_s, y2_r, y_dev)
    ex_z2 = exchange(nz, my_z, c2, r2z, z2_s, z2_r, z_dev)

    ex_y1[0]()
    ex_x2[0]()
    ex_y1[1]()

    @pl.loop(0, nz)
    def _(z):
        for x in range(nx):
            b1[x, z] = ex_y1[3](x, z)

    ex_x1[0]()
    ex_x2[1]()

    @pl.loop(0, nz)
    def _(z):
        for y in range(ny):
            b2[y, z] = ex_x2[3](y, z)

    ex_y2[0]()
    ex_x1[1]()

    @pl.loop(0, nz)
    def _(z):
        c1[z] = ex_x1[3](z)

    ex_z1[0]()
    ex_y2[1]()

    @pl.loop(0, nz)
    def _(z):
        c2[z] = ex_y2[3](z)

    ex_z2[0]()
    ex_z1[1]()
    fin[0] = ex_z1[3]()
    ex_z2[1]()
    fin[1] = ex_z2[3]()

    def ag_copy(p, src):
        return remote(fin, gath.at[src], ag_s.at[p], ag_r.at[src], grp_dev(p))

    for i in range(1, ngrp):
        ag_copy(lax.rem(g + i, ngrp), g).start()
    gath[g] = fin[...]

    @pl.loop(1, n)
    def _(i):
        p = to(i)
        req_copy(p, me).wait_send()
        fwd_copy(p, me).wait_send()
        bwd_copy(p, me).wait_send()

    @pl.loop(0, n)
    def _(b):
        core_copy(b).wait_send()

    for ex in (ex_y1, ex_x1, ex_z1, ex_x2, ex_y2, ex_z2):
        ex[2]()

    for i in range(1, ngrp):
        p = lax.rem(g + i, ngrp)
        ag_copy(p, p).wait_recv()
    for c in range(2):
        for y in range(ny):
            for h in range(2):
                r0 = ((c * ny + y) * 2 + h) * rows
                piece = gath[y * 2 + c, h].astype(F32)
                wog_ref[r0 : r0 + rows, :] = piece[:, 0:width]
                tmp[r0 : r0 + rows, :] = piece[:, width:]
    wig_ref[...] = tmp[...].T
    for i in range(1, ngrp):
        ag_copy(lax.rem(g + i, ngrp), g).wait_send()


def local(n, ngrp, queries, positive, item_feats, frequency, samples, counts, w_in, w_out):
    nx = max(1, math.isqrt(n // 2))
    nz = n // nx
    ny = ngrp // 2
    slots = samples.shape[2]
    items, feat = item_feats.shape
    nq, width = queries.shape
    cb = w_out.shape[0] // n
    rows = cb // (4 * ny)
    lanes = width + feat
    dma = lambda k: pltpu.SemaphoreType.DMA((k,))
    vm = lambda *s: pltpu.VMEM(s, BF16)
    vf = lambda *s: pltpu.VMEM(s, F32)
    vspec = pl.BlockSpec(memory_space=pltpu.VMEM)
    return pl.pallas_call(
        functools.partial(kernel, (n, ngrp, nx, nz, ny, rows)),
        out_shape=(
            jax.ShapeDtypeStruct((nq, width), F32),
            jax.ShapeDtypeStruct((feat, cb), F32),
            jax.ShapeDtypeStruct((cb, width), F32),
        ),
        in_specs=[vspec] * 5 + [pl.BlockSpec(memory_space=pltpu.SMEM)] + [vspec] * 2,
        out_specs=(vspec,) * 3,
        scratch_shapes=[
            pltpu.VMEM((n, 1, slots), jnp.int32),
            vm(n, slots + 16, width), vm(n, slots + 16, width),
            vm(n, nq, slots), vf(n, nq, slots), vf(nq, slots),
            vm(n, slots, width), vm(n, slots, width),
            vm(n, items, cb), vm(n, cb, items),
            vf(items, width), vf(nq, width),
            vm(n, 2, ny, 2, rows, lanes), vm(n, ny, 2, rows, lanes),
            vm(ny, nx, nz, rows, lanes), vm(ny, nx, nz, rows, lanes),
            vm(nx, nz, rows, lanes), vm(nx, nz, rows, lanes),
            vm(nz, rows, lanes), vm(nz, rows, lanes),
            vm(nx, ny, nz, rows, lanes), vm(nx, ny, nz, rows, lanes),
            vm(ny, nz, rows, lanes), vm(ny, nz, rows, lanes),
            vm(nz, rows, lanes), vm(nz, rows, lanes),
            vm(2, rows, lanes), vm(ngrp, 2, rows, lanes), vf(cb, feat),
            dma(n), dma(n), dma(n), dma(n), dma(n), dma(n), dma(n), dma(n),
            dma(ny), dma(ny), dma(nx), dma(nx), dma(nz), dma(nz),
            dma(nx), dma(nx), dma(ny), dma(ny), dma(nz), dma(nz), dma(ngrp), dma(ngrp),
        ],
        compiler_params=pltpu.CompilerParams(
            collective_id=0, has_side_effects=True, vmem_limit_bytes=56 * 1024 * 1024
        ),
    )(
        queries,
        positive.reshape(1, nq),
        item_feats,
        frequency.reshape(1, items),
        samples.reshape(n, 1, slots),
        counts,
        w_in,
        w_out,
    )


def solution(mesh):
    in_specs = (
        P(("grp", "shard"), None),
        P(("grp", "shard")),
        P(("grp", "shard"), None),
        P(("grp", "shard")),
        P(("grp", "shard"), None, None),
        P(("grp", "shard"), None),
        P(),
        P(),
    )
    out_specs = (P(("grp", "shard"), None), P(None, "shard"), P("shard", None))
    body = functools.partial(local, mesh.shape["shard"], mesh.shape["grp"])
    return jax.shard_map(body, mesh=mesh, in_specs=in_specs, out_specs=out_specs, check_vma=False)
```

time: 272 us -> 82.5 us (0.30)
  waiting for transfers between devices: 173 us -> 0 us
  Pallas kernels: 0 us -> 75.9 us
  blocking collectives: 21 us -> 0 us
  matrix products: 17.2 us -> 0 us
  local copies, waits for them, and re-layouts: 21 us -> 5.21 us
  other arithmetic: 13.8 us -> 0 us
  between operations: 14.1 us -> 0.64 us
  starting transfers between devices: 10.9 us -> 0 us
    reduce_scatter x2 -> x0, waiting for transfers between devices: 129 us -> none  [the longest x1 70.6 us: local(): lax.psum_scatter(w_out_part.astype(jnp.bfloat16), 'shard', scatter_dimens...]
    pallas_call x0 -> x1, Pallas kernels: none -> 75.9 us  [local(): pl.pallas_call(functools.partial(kernel, (n, ngrp, nx, nz, ny, rows)), ou...]
    psum x1 -> x0, waiting for transfers between devices: 33.3 us -> none  [local(): lax.psum(w_in_share.astype(jnp.bfloat16), 'grp').astype(jnp.float32)]
    all_gather x1 -> x0, blocking collectives: 21 us -> none  [local(): lax.all_gather(log_bias, 'shard', axis=0, tiled=True)]
    dot_general x7 -> x0, matrix products: 17.2 us -> none  [the longest x3 9.95 us: contract_rows(): lax.dot_general(left, right, (((0,), (0,)), ((), ())), preferred_element_...]
    gather x4 -> x0, local copies, waits for them, and re-layouts: 13 us -> none  [the longest x1 6.8 us: local(): neg_bias = jnp.take(group_bias, flat_index, axis=0)]
    all_to_all x2 -> x0, starting transfers between devices: 10.8 us -> none  [the longest x1 7.26 us: local(): lax.all_to_all(own_samples, 'shard', split_axis=0, concat_axis=0, tiled=T...]
    scatter-add x2 -> x0, other arithmetic: 8.72 us -> none  [the longest x1 6.3 us: local(): jax.ops.segment_sum(returned.reshape(-1, emb_width).astype(jnp.float32),...]
  transfers between devices with their start and end apart: 6 -> 0, of which waited for: 5 -> 0; matrix products, arithmetic and copies ran while one was open for 12% -> 0% of each run, Pallas kernels for 0% -> 0%
where the time goes in v1:
time: 82.5 us; the launch traced here: 81.8 us
  Pallas kernels  75.9 us (92%)
  local copies, waits for them, and re-layouts  5.21 us (6%)
    pallas_call x1, Pallas kernels, local(): pl.pallas_call(functools.partial(kernel, (n, ngrp, nx, nz, ny, rows)), ou...  75.9 us
    unnamed x3, local copies, waits for them, and re-layouts  5.21 us

profile of v1, /device:TPU:0, one launch (start us, length us, event | category | flops | bytes accessed | tf_op | source)
XLA Modules:
  0.0 81.8 jit_solution(5905552247787092046)
XLA Ops:
  0.6 75.9 %shard_map.103 = (f32[256,256]{1,0:T(8,128)}, f32[128,512]{1,0:T(8,128)}, f32[512,256]{1,0:T(8,128)}) custom-call(bf16[256,256]{1,0:T(8,128)(2,1)} %q_ref.1, s32[1,256]{1,0:T(1,128)} %bitcast.4, bf16[256,128]{1,0:T(8,128)(2,1)} %feats_ref.1, s32[1,256]{1,0:T(1,128)} %bitcast.5, s32[8,1,128]{2,1,0:T(1,128)} %bitcast.3, s32[1,8]{1,0:T(1,128)} %counts_ref.1, ...), custom_call_target="tpu_custom_call" | custom-call | tf_op jit(solution)/shard_map/pallas_call | solution.py:373
  76.6 1.7 %copy.14 = f32[256,256]{1,0:T(8,128)} copy(f32[256,256]{1,0:T(8,128)} %get-tuple-element.6) | data formatting | bytes 524288
  78.3 1.7 %copy.15 = f32[128,512]{1,0:T(8,128)} copy(f32[128,512]{1,0:T(8,128)} %get-tuple-element.7) | data formatting | bytes 524288
  79.9 1.9 %copy.16 = f32[512,256]{1,0:T(8,128)} copy(f32[512,256]{1,0:T(8,128)} %get-tuple-element.8) | data formatting | bytes 1048576

commit v2 on v1

v2 whole, which is shorter than its diff:
```python
import functools
import math

import jax
import jax.numpy as jnp
from jax import lax
from jax.experimental import pallas as pl
from jax.experimental.pallas import tpu as pltpu
from jax.sharding import PartitionSpec as P

inv_temperature = 1.0 / 0.05
log_base = 4.0
epsilon = 1e-06
masked_logit = -10000.0
MESH = pl.DeviceIdType.MESH
F32 = jnp.float32
BF16 = jnp.bfloat16


def mm(left, right, dims):
    return lax.dot_general(left, right, (dims, ((), ())), preferred_element_type=F32)


NN = ((1,), (0,))
NT = ((1,), (1,))
TN = ((0,), (0,))


def kernel(
    dims,
    q_ref, pos_ref, feats_ref, freq_ref, samp_ref, counts_ref, w_in_ref, w_out_ref,
    qg_ref, sum_ref,
    req, fall, uall, rall, neg, ngrad, esc, tot, rsend, rrecv, hidt, wt, acc, uq,
    woacc, wiacc, part, crecv, yall, gath,
    req_s, req_r, bwd_s, bwd_r, core_s, core_r, y_s, y_r, ag_s, ag_r, *ag_sems,
):
    n, ngrp, nx, nz, ny = dims
    width = w_out_ref.shape[1]
    items = feats_ref.shape[0]
    slots = samp_ref.shape[2]
    cb = w_out_ref.shape[0] // n
    g = lax.axis_index("grp")
    me = lax.axis_index("shard")
    core, my_y = lax.rem(g, 2), lax.div(g, 2)
    my_x, my_z = lax.rem(me, nx), lax.div(me, nx)

    def shard_dev(p):
        return {"shard": p}

    def grp_dev(p):
        return {"grp": p}

    def remote(src, dst, ssem, rsem, dev):
        return pltpu.make_async_remote_copy(
            src_ref=src, dst_ref=dst, send_sem=ssem, recv_sem=rsem,
            device_id=dev, device_id_type=MESH,
        )

    class Gather:
        def __init__(self, buf, split, sems):
            self.buf, self.sems, self.sent = buf, sems, []
            self.parts = (pl.ds(0, split), pl.ds(split, buf.shape[1] - split))

        def copy(self, h, block, ssem, dev):
            ref = self.buf.at[block, self.parts[h]]
            return remote(ref, ref, ssem, self.sems[0].at[h, block], dev)

        def send(self, cond, h, block, kind, dev, x=0):
            ssem = self.sems[kind].at[(h, x, block) if kind == 3 else (h, block)]
            make = lambda: self.copy(h, block, ssem, dev)
            pl.when(cond)(lambda: make().start())
            self.sent.append((cond, make))

        def right(self, cond, h, block):
            self.send(cond & (my_z + 1 < nz), h, block, 1, shard_dev(lax.min(me + nx, n - 1)))

        def left(self, cond, h, block):
            self.send(cond & (my_z >= 1), h, block, 2, shard_dev(lax.max(me - nx, 0)))

        def across(self, cond, h, block):
            for i in range(1, nx):
                x = lax.rem(my_x + i, nx)
                self.send(cond, h, block, 3, shard_dev(my_z * nx + x), x)

        def wait(self, cond, h, block):
            pl.when(cond)(
                lambda: self.copy(h, block, self.sems[1].at[h, block], shard_dev(me)).wait_recv()
            )

        def start(self):
            yes = my_z >= 0
            self.right(yes, 0, me)
            self.left(yes, 0, me)
            self.across(yes, 1, me)
            self.across(yes, 0, me)
            self.right(yes, 1, me)
            self.left(yes, 1, me)

        def step(self, k):
            yes = my_z >= 0
            lo, hi = my_z - k >= 0, my_z + k < nz
            zl, zh = lax.max(my_z - k, 0), lax.min(my_z + k, nz - 1)
            if k == 1:
                for i in range(1, nx):
                    block = my_z * nx + lax.rem(my_x + i, nx)
                    self.wait(yes, 1, block)
                    self.right(yes, 1, block)
                    self.left(yes, 1, block)
            for cond, z, onward in ((lo, zl, self.right), (hi, zh, self.left)):
                block = z * nx + my_x
                self.wait(cond, 0, block)
                onward(cond, 0, block)
                self.across(cond, 0, block)
            for i in range(nx):
                for cond, z, onward in ((lo, zl, self.right), (hi, zh, self.left)):
                    block = z * nx + lax.rem(my_x + i, nx)
                    self.wait(cond, 1, block)
                    onward(cond, 1, block)

        def finish(self, z):
            for i in range(1, nx):
                self.wait(my_z >= 0, 0, z * nx + lax.rem(my_x + i, nx))

        def drain(self):
            for cond, make in self.sent:
                pl.when(cond)(lambda: make().wait_send())

        def run(self, work):
            for k in range(1, nz):
                self.step(k)
                for cond, z in (
                    (my_z - k >= 0, lax.max(my_z - k, 0)),
                    (my_z + k < nz, lax.min(my_z + k, nz - 1)),
                ):
                    pl.when(cond)(lambda: work(z * nx + my_x))
            for i in range(1, nx):
                x = lax.rem(my_x + i, nx)

                @pl.loop(0, nz)
                def _(k):
                    z = lax.rem(my_z + k, nz)
                    self.wait(my_z >= 0, 0, z * nx + x)
                    work(z * nx + x)

    barrier = pltpu.get_barrier_semaphore()
    for i in range(1, n):
        pl.semaphore_signal(
            barrier, inc=1, device_id=shard_dev(lax.rem(me + i, n)), device_id_type=MESH
        )
    for i in range(1, ngrp):
        pl.semaphore_signal(
            barrier, inc=1, device_id=grp_dev(lax.rem(g + i, ngrp)), device_id_type=MESH
        )
    fall[me] = feats_ref[...]
    pl.semaphore_wait(barrier, n - 1 + ngrp - 1)

    def req_copy(p, src):
        return remote(samp_ref.at[p], req.at[src], req_s.at[p], req_r.at[src], shard_dev(p))

    def bwd_copy(p, src):
        return remote(rsend.at[p], rrecv.at[src], bwd_s.at[p], bwd_r.at[src], shard_dev(p))

    def to(i):
        return lax.rem(me + i, n)

    def frm(i):
        return lax.rem(me + n - i, n)

    ag_f = Gather(fall, items // 2, ag_sems[0:4])
    ag_u = Gather(uall, items // 2 + 16, ag_sems[4:8])
    ag_r_ = Gather(rall, items // 2, ag_sems[8:12])

    ag_f.start()

    @pl.loop(1, n)
    def _(i):
        req_copy(to(i), me).start()

    req[pl.ds(me, 1)] = samp_ref[pl.ds(me, 1)]

    acc[...] = jnp.zeros_like(acc)
    for k in range(nz):
        if k > 0:
            ag_f.step(k)

        @pl.loop(k * nx, (k + 1) * nx)
        def _(b):
            cols = pl.ds(pl.multiple_of(b * cb, 128), cb)
            pre = mm(feats_ref[...], w_in_ref[:, cols], NN)
            h = jnp.maximum(pre, 0.0).astype(BF16)
            acc[...] += mm(h, w_out_ref[cols, :], NN)

    raw_emb = acc[...]
    radius = jnp.sqrt(jnp.sum(raw_emb * raw_emb, -1, keepdims=True) + epsilon)
    unit = raw_emb / radius
    unit_bf = unit.astype(BF16)
    bias = (log_base - jnp.log(freq_ref[...].astype(F32) + 1.0)).astype(BF16)
    uall[me, 0:items, :] = unit_bf
    uall[me, items:, :] = jnp.broadcast_to(bias.astype(F32), (16, items)).astype(BF16)
    ag_u.start()

    queries = q_ref[...].astype(F32)
    query_norm = jnp.sqrt(jnp.sum(queries * queries, -1, keepdims=True) + epsilon)
    query_unit = queries / query_norm
    query_bf = query_unit.astype(BF16)
    pos_pick = (
        lax.broadcasted_iota(jnp.int32, (items, q_ref.shape[0]), 0) == pos_ref[...]
    ).astype(F32).astype(BF16)
    pos_rows = mm(pos_pick, unit_bf, TN)
    pos_logit = jnp.sum(query_bf.astype(F32) * pos_rows, -1, keepdims=True) * inv_temperature
    pos_exp = jnp.exp(pos_logit)

    item_iota = lax.broadcasted_iota(jnp.int32, (items, slots), 0)
    slot_iota = lax.broadcasted_iota(jnp.int32, (1, slots), 1)

    def onehot(row):
        return (item_iota == row).astype(F32).astype(BF16)

    tot[...] = jnp.zeros_like(tot)

    def logits(src):
        pick = onehot(samp_ref[src])
        rows = mm(pick, uall[src, 0:items, :], TN).astype(BF16)
        neg[src] = rows
        off = mm(uall[src, items:, :], pick, NN)[0:1]
        off = jnp.where(slot_iota < counts_ref[0, src], off, masked_logit)
        e = jnp.exp(mm(query_bf, rows, NT) * inv_temperature + off)
        esc[src] = e
        tot[...] += e

    logits(me)
    ag_u.run(logits)

    total = pos_exp + jnp.sum(tot[...], -1, keepdims=True)
    scale = inv_temperature / total
    pos_grad = (pos_exp / total - 1.0) * inv_temperature

    def row_grads(src):
        d = (esc[src] * scale).astype(BF16)
        ngrad[src] = d
        return mm(d, query_bf, TN).astype(BF16)

    @pl.loop(1, n)
    def _(i):
        p = to(i)
        rsend[p] = row_grads(p)
        bwd_copy(p, me).start()

    rrecv[me] = row_grads(me)

    uq[...] = pos_grad * pos_rows

    @pl.loop(0, n)
    def _(b):
        uq[...] += mm(ngrad[b], neg[b], NN)

    unit_qgrad = uq[...]
    qg_ref[...] = (
        unit_qgrad - query_unit * jnp.sum(query_unit * unit_qgrad, -1, keepdims=True)
    ) / query_norm

    for z in range(nz):
        ag_f.finish(z)
    wt[...] = w_in_ref[:, pl.ds(pl.multiple_of(me * cb, 128), cb)].astype(F32).T.astype(BF16)

    @pl.loop(0, n)
    def _(b):
        hidt[b] = jnp.maximum(mm(wt[...], fall[b], NT), 0.0).astype(BF16)

    pos_term = pos_grad * query_bf.astype(F32)
    high = pos_term.astype(BF16)
    low = (pos_term - high.astype(F32)).astype(BF16)
    acc[...] = mm(pos_pick, high, NN) + mm(pos_pick, low, NN)
    acc[...] += mm(onehot(req[me]), rrecv[me], NN)

    @pl.loop(1, n)
    def _(i):
        src = frm(i)
        req_copy(src, src).wait_recv()
        pick = onehot(req[src])
        bwd_copy(src, src).wait_recv()
        acc[...] += mm(pick, rrecv[src], NN)

    item_grad = acc[...]
    rall[me] = (
        (item_grad - unit * jnp.sum(unit * item_grad, -1, keepdims=True)) / radius
    ).astype(BF16)
    ag_r_.start()

    woacc[...] = jnp.zeros_like(woacc)
    wiacc[...] = jnp.zeros_like(wiacc)
    block_rows = pl.ds(pl.multiple_of(me * cb, cb), cb)

    def weights(src):
        raw = rall[src]
        ht = hidt[src]
        hg = mm(w_out_ref[block_rows, :], raw, NT)
        pg = jnp.where(ht.astype(F32) > 0.0, hg, 0.0).astype(BF16)
        woacc[...] += mm(ht, raw, NN)
        wiacc[...] += mm(pg, fall[src], NN)

    weights(me)
    ag_r_.run(weights)

    half = cb // 2
    for c in range(2):
        part[c, :, 0:width] = woacc[c * half : (c + 1) * half].astype(BF16)
        part[c, :, width:] = wiacc[c * half : (c + 1) * half].astype(BF16)
    other = grp_dev(g + 1 - 2 * core)
    core_copy = remote(part.at[1 - core], crecv, core_s.at[0], core_r.at[0], other)
    core_copy.start()
    core_copy.wait_recv()
    yall[my_y] = (part[core].astype(F32) + crecv[...].astype(F32)).astype(BF16)

    def y_copy(p, slot):
        return remote(yall.at[my_y], yall.at[slot], y_s.at[p], y_r.at[slot], grp_dev(p * 2 + core))

    for i in range(1, ny):
        y_copy(lax.rem(my_y + i, ny), my_y).start()

    @pl.loop(1, n)
    def _(i):
        p = to(i)
        req_copy(p, me).wait_send()
        bwd_copy(p, me).wait_send()

    core_copy.wait_send()
    for ag in (ag_f, ag_u, ag_r_):
        ag.drain()

    for i in range(1, ny):
        p = lax.rem(my_y + i, ny)
        y_copy(p, p).wait_recv()
    value = yall[0].astype(F32)
    for y in range(1, ny):
        value += yall[y].astype(F32)
    gath[core] = value.astype(BF16)
    ag_copy = remote(gath.at[core], gath.at[core], ag_s.at[0], ag_r.at[0], other)
    ag_copy.start()
    for i in range(1, ny):
        y_copy(lax.rem(my_y + i, ny), my_y).wait_send()
    sum_ref[core] = gath[core]
    remote(gath.at[1 - core], gath.at[1 - core], ag_s.at[0], ag_r.at[0], other).wait_recv()
    sum_ref[1 - core] = gath[1 - core]
    ag_copy.wait_send()


def finish(qg_ref, sum_ref, qo_ref, wig_ref, wog_ref):
    half, width = sum_ref.shape[1], wog_ref.shape[1]
    qo_ref[...] = qg_ref[...]
    block = jnp.concatenate([sum_ref[0].astype(F32), sum_ref[1].astype(F32)], 0)
    wog_ref[...] = block[:, 0:width]
    wig_ref[...] = block[:, width:].T


def local(n, ngrp, queries, positive, item_feats, frequency, samples, counts, w_in, w_out):
    nx = max(1, math.isqrt(n // 2))
    nz = n // nx
    ny = ngrp // 2
    slots = samples.shape[2]
    items, feat = item_feats.shape
    nq, width = queries.shape
    cb = w_out.shape[0] // n
    lanes = width + feat
    dma = lambda *k: pltpu.SemaphoreType.DMA(k)
    vm = lambda *s: pltpu.VMEM(s, BF16)
    vf = lambda *s: pltpu.VMEM(s, F32)
    vspec = pl.BlockSpec(memory_space=pltpu.VMEM)
    query_grad, sums = pl.pallas_call(
        functools.partial(kernel, (n, ngrp, nx, nz, ny)),
        out_shape=(
            jax.ShapeDtypeStruct((nq, width), F32),
            jax.ShapeDtypeStruct((2, cb // 2, lanes), BF16),
        ),
        in_specs=[vspec] * 5 + [pl.BlockSpec(memory_space=pltpu.SMEM)] + [vspec] * 2,
        out_specs=(vspec,) * 2,
        scratch_shapes=[
            pltpu.VMEM((n, 1, slots), jnp.int32),
            vm(n, items, feat), vm(n, items + 16, width), vm(n, items, width),
            vm(n, slots, width), vm(n, nq, slots), vf(n, nq, slots), vf(nq, slots),
            vm(n, slots, width), vm(n, slots, width),
            vm(n, cb, items), vm(cb, feat), vf(items, width), vf(nq, width),
            vf(cb, width), vf(cb, feat),
            vm(2, cb // 2, lanes), vm(cb // 2, lanes), vm(ny, cb // 2, lanes), vm(2, cb // 2, lanes),
            dma(n), dma(n), dma(n), dma(n), dma(1), dma(1), dma(ny), dma(ny), dma(1), dma(1),
        ]
        + [dma(2, n), dma(2, n), dma(2, n), dma(2, nx, n)] * 3,
        compiler_params=pltpu.CompilerParams(
            collective_id=0, has_side_effects=True, vmem_limit_bytes=56 * 1024 * 1024
        ),
    )(
        queries,
        positive.reshape(1, nq),
        item_feats,
        frequency.reshape(1, items),
        samples.reshape(n, 1, slots),
        counts,
        w_in,
        w_out,
    )
    return pl.pallas_call(
        finish,
        out_shape=(
            jax.ShapeDtypeStruct((nq, width), F32),
            jax.ShapeDtypeStruct((feat, cb), F32),
            jax.ShapeDtypeStruct((cb, width), F32),
        ),
        in_specs=[vspec] * 2,
        out_specs=(vspec,) * 3,
    )(query_grad, sums)


def solution(mesh):
    in_specs = (
        P(("grp", "shard"), None),
        P(("grp", "shard")),
        P(("grp", "shard"), None),
        P(("grp", "shard")),
        P(("grp", "shard"), None, None),
        P(("grp", "shard"), None),
        P(),
        P(),
    )
    out_specs = (P(("grp", "shard"), None), P(None, "shard"), P("shard", None))
    body = functools.partial(local, mesh.shape["shard"], mesh.shape["grp"])
    return jax.shard_map(body, mesh=mesh, in_specs=in_specs, out_specs=out_specs, check_vma=False)
```

time: 82.5 us -> 78.4 us (0.950)
  local copies, waits for them, and re-layouts: 5.21 us -> 0 us
  Pallas kernels: 75.9 us -> 77.6 us
    unnamed x3 -> x0, local copies, waits for them, and re-layouts: 5.21 us -> none
    pallas_call x1 -> x2, Pallas kernels: 75.9 us -> 77.6 us  [the longest x1 75.5 us: local(): pl.pallas_call(functools.partial(kernel, (n, ngrp, nx, nz, ny)), out_shap...]
where the time goes in v2:
time: 78.4 us; the launch traced here: 78.2 us
  Pallas kernels  77.6 us (99%)
    pallas_call x1, Pallas kernels, local(): pl.pallas_call(functools.partial(kernel, (n, ngrp, nx, nz, ny)), out_shap...  75.5 us
    pallas_call x1, Pallas kernels, local(): pl.pallas_call(finish, out_shape=(jax.ShapeDtypeStruct((nq, width), F32),...  2.08 us

profile of v2, /device:TPU:0, one launch (start us, length us, event | category | flops | bytes accessed | tf_op | source)
XLA Modules:
  0.0 78.2 jit_solution(8908574509803856214)
XLA Ops:
  0.6 75.5 %shard_map.103 = (f32[256,256]{1,0:T(8,128)}, bf16[2,256,384]{2,1,0:T(8,128)(2,1)}) custom-call(bf16[256,256]{1,0:T(8,128)(2,1)} %q_ref.1, s32[1,256]{1,0:T(1,128)} %bitcast.4, bf16[256,128]{1,0:T(8,128)(2,1)} %feats_ref.1, s32[1,256]{1,0:T(1,128)} %bitcast.5, s32[8,1,128]{2,1,0:T(1,128)} %bitcast.3, s32[1,8]{1,0:T(1,128)} %counts_ref.1, ...), custom_call_target="tpu_custom_call" | custom-call | tf_op jit(solution)/shard_map/pallas_call | solution.py:369
  76.1 2.1 %shard_map.104 = (f32[256,256]{1,0:T(8,128)}, f32[128,512]{1,0:T(8,128)}, f32[512,256]{1,0:T(8,128)}) custom-call(f32[256,256]{1,0:T(8,128)} %get-tuple-element.5.qg_ref, bf16[2,256,384]{2,1,0:T(8,128)(2,1)} %get-tuple-element.6.sum_ref), custom_call_target="tpu_custom_call" | custom-call | tf_op jit(solution)/shard_map/pallas_call | solution.py:401

commit v3 on v2

--- a/solution.py
+++ b/solution.py
@@ -35,6 +35,7 @@
     req_s, req_r, bwd_s, bwd_r, core_s, core_r, y_s, y_r, ag_s, ag_r, *ag_sems,
 ):
     n, ngrp, nx, nz, ny = dims
+    few = n <= 8
     width = w_out_ref.shape[1]
     items = feats_ref.shape[0]
     slots = samp_ref.shape[2]
@@ -166,9 +167,9 @@
     def frm(i):
         return lax.rem(me + n - i, n)
 
-    ag_f = Gather(fall, items // 2, ag_sems[0:4])
-    ag_u = Gather(uall, items // 2 + 16, ag_sems[4:8])
-    ag_r_ = Gather(rall, items // 2, ag_sems[8:12])
+    ag_f = Gather(fall, items // 4 * 3, ag_sems[0:4])
+    ag_u = Gather(uall, items // 4 * 3 + 16, ag_sems[4:8])
+    ag_r_ = Gather(rall, items // 4 * 3, ag_sems[8:12])
 
     ag_f.start()
 
@@ -180,10 +181,10 @@
 
     acc[...] = jnp.zeros_like(acc)
     for k in range(nz):
-        if k > 0:
-            ag_f.step(k)
-
-        @pl.loop(k * nx, (k + 1) * nx)
+        if k == nz // 2:
+            ag_f.step(1)
+
+        @pl.loop(k * nx, (k + 1) * nx, unroll=True)
         def _(b):
             cols = pl.ds(pl.multiple_of(b * cb, 128), cb)
             pre = mm(feats_ref[...], w_in_ref[:, cols], NN)
@@ -197,6 +198,8 @@
     bias = (log_base - jnp.log(freq_ref[...].astype(F32) + 1.0)).astype(BF16)
     uall[me, 0:items, :] = unit_bf
     uall[me, items:, :] = jnp.broadcast_to(bias.astype(F32), (16, items)).astype(BF16)
+    if nz > 2:
+        ag_f.step(2)
     ag_u.start()
 
     queries = q_ref[...].astype(F32)
@@ -210,6 +213,9 @@
     pos_logit = jnp.sum(query_bf.astype(F32) * pos_rows, -1, keepdims=True) * inv_temperature
     pos_exp = jnp.exp(pos_logit)
 
+    for k in range(3, nz):
+        ag_f.step(k)
+
     item_iota = lax.broadcasted_iota(jnp.int32, (items, slots), 0)
     slot_iota = lax.broadcasted_iota(jnp.int32, (1, slots), 1)
 
@@ -240,7 +246,7 @@
         ngrad[src] = d
         return mm(d, query_bf, TN).astype(BF16)
 
-    @pl.loop(1, n)
+    @pl.loop(1, n, unroll=few)
     def _(i):
         p = to(i)
         rsend[p] = row_grads(p)
@@ -250,7 +256,7 @@
 
     uq[...] = pos_grad * pos_rows
 
-    @pl.loop(0, n)
+    @pl.loop(0, n, unroll=few)
     def _(b):
         uq[...] += mm(ngrad[b], neg[b], NN)
 
@@ -263,7 +269,7 @@
         ag_f.finish(z)
     wt[...] = w_in_ref[:, pl.ds(pl.multiple_of(me * cb, 128), cb)].astype(F32).T.astype(BF16)
 
-    @pl.loop(0, n)
+    @pl.loop(0, n, unroll=few)
     def _(b):
         hidt[b] = jnp.maximum(mm(wt[...], fall[b], NT), 0.0).astype(BF16)
 

time: 78.4 us -> 74 us (0.944)
  Pallas kernels: 77.6 us -> 73.3 us
    pallas_call x1, Pallas kernels: 75.5 us -> 71.2 us  [local(): pl.pallas_call(functools.partial(kernel, (n, ngrp, nx, nz, ny)), out_shap...]
where the time goes in v3:
time: 74 us; the launch traced here: 73.9 us
  Pallas kernels  73.3 us (99%)
    pallas_call x1, Pallas kernels, local(): pl.pallas_call(functools.partial(kernel, (n, ngrp, nx, nz, ny)), out_shap...  71.2 us
    pallas_call x1, Pallas kernels, local(): pl.pallas_call(finish, out_shape=(jax.ShapeDtypeStruct((nq, width), F32),...  2.08 us

profile of v3, /device:TPU:0, one launch (start us, length us, event | category | flops | bytes accessed | tf_op | source)
XLA Modules:
  0.0 73.9 jit_solution(8867066527202251028)
XLA Ops:
  0.6 71.2 %shard_map.103 = (f32[256,256]{1,0:T(8,128)}, bf16[2,256,384]{2,1,0:T(8,128)(2,1)}) custom-call(bf16[256,256]{1,0:T(8,128)(2,1)} %q_ref.1, s32[1,256]{1,0:T(1,128)} %bitcast.4, bf16[256,128]{1,0:T(8,128)(2,1)} %feats_ref.1, s32[1,256]{1,0:T(1,128)} %bitcast.5, s32[8,1,128]{2,1,0:T(1,128)} %bitcast.3, s32[1,8]{1,0:T(1,128)} %counts_ref.1, ...), custom_call_target="tpu_custom_call" | custom-call | tf_op jit(solution)/shard_map/pallas_call | solution.py:375
  71.8 2.1 %shard_map.104 = (f32[256,256]{1,0:T(8,128)}, f32[128,512]{1,0:T(8,128)}, f32[512,256]{1,0:T(8,128)}) custom-call(f32[256,256]{1,0:T(8,128)} %get-tuple-element.5.qg_ref, bf16[2,256,384]{2,1,0:T(8,128)(2,1)} %get-tuple-element.6.sum_ref), custom_call_target="tpu_custom_call" | custom-call | tf_op jit(solution)/shard_map/pallas_call | solution.py:407

commit v4 on v3

--- a/solution.py
+++ b/solution.py
@@ -167,9 +167,9 @@
     def frm(i):
         return lax.rem(me + n - i, n)
 
-    ag_f = Gather(fall, items // 4 * 3, ag_sems[0:4])
-    ag_u = Gather(uall, items // 4 * 3 + 16, ag_sems[4:8])
-    ag_r_ = Gather(rall, items // 4 * 3, ag_sems[8:12])
+    ag_f = Gather(fall, items // 2, ag_sems[0:4])
+    ag_u = Gather(uall, items // 2 + 16, ag_sems[4:8])
+    ag_r_ = Gather(rall, items // 2, ag_sems[8:12])
 
     ag_f.start()
 

time: 74 us -> 77.7 us (1.050)
  Pallas kernels: 73.3 us -> 76.9 us
    pallas_call x1, Pallas kernels: 71.2 us -> 74.8 us  [local(): pl.pallas_call(functools.partial(kernel, (n, ngrp, nx, nz, ny)), out_shap...]
where the time goes in v4:
time: 77.7 us; the launch traced here: 77.5 us
  Pallas kernels  76.9 us (99%)
    pallas_call x1, Pallas kernels, local(): pl.pallas_call(functools.partial(kernel, (n, ngrp, nx, nz, ny)), out_shap...  74.8 us
    pallas_call x1, Pallas kernels, local(): pl.pallas_call(finish, out_shape=(jax.ShapeDtypeStruct((nq, width), F32),...  2.08 us

profile of v4, /device:TPU:0, one launch (start us, length us, event | category | flops | bytes accessed | tf_op | source)
XLA Modules:
  0.0 77.5 jit_solution(16192496974356172490)
XLA Ops:
  0.6 74.8 %shard_map.103 = (f32[256,256]{1,0:T(8,128)}, bf16[2,256,384]{2,1,0:T(8,128)(2,1)}) custom-call(bf16[256,256]{1,0:T(8,128)(2,1)} %q_ref.1, s32[1,256]{1,0:T(1,128)} %bitcast.4, bf16[256,128]{1,0:T(8,128)(2,1)} %feats_ref.1, s32[1,256]{1,0:T(1,128)} %bitcast.5, s32[8,1,128]{2,1,0:T(1,128)} %bitcast.3, s32[1,8]{1,0:T(1,128)} %counts_ref.1, ...), custom_call_target="tpu_custom_call" | custom-call | tf_op jit(solution)/shard_map/pallas_call | solution.py:375
  75.4 2.1 %shard_map.104 = (f32[256,256]{1,0:T(8,128)}, f32[128,512]{1,0:T(8,128)}, f32[512,256]{1,0:T(8,128)}) custom-call(f32[256,256]{1,0:T(8,128)} %get-tuple-element.5.qg_ref, bf16[2,256,384]{2,1,0:T(8,128)(2,1)} %get-tuple-element.6.sum_ref), custom_call_target="tpu_custom_call" | custom-call | tf_op jit(solution)/shard_map/pallas_call | solution.py:407
